TPU v7x, 32 devices: a whole 2x2x4 slice. The times are simulated.
32 devices in a mesh: dp: 4 (over z), ctx: 2 (over x), tp: 4 (over y, core).
Axes of the slice: x: 2, y: 2, z: 4, core: 2. Of those that a mesh axis runs over, the one named last changes fastest.
Arguments:
- tokens: bfloat16 [512, 2048], P(('dp', 'ctx', 'tp')), may hold values from -6 to 6
- grad_out: bfloat16 [512, 2048], P(('dp', 'ctx', 'tp')), may hold values from -6 to 6
- expert_ids: int32 [512, 8], P(('dp', 'ctx')), may hold values from 0 to 63, all different within a row; in each aligned block of 64 rows (0 to 63, 64 to 127, ...) at most 16 rows name the same one
- router_weights: bfloat16 [512, 8], P(('dp', 'ctx')), may hold values from 0.029907227 to 0.3984375
- w_gate: bfloat16 [64, 2048, 1536], P(('dp', 'ctx'), None, 'tp'), may hold values from -0.125 to 0.125
- w_up: bfloat16 [64, 2048, 1536], P(('dp', 'ctx'), None, 'tp'), may hold values from -0.125 to 0.125
- w_down: bfloat16 [64, 1536, 2048], P(('dp', 'ctx'), 'tp'), may hold values from -0.15625 to 0.15625
Outputs:
- layer_out: bfloat16 [512, 2048], P(('dp', 'ctx', 'tp'))
- grad_tokens: bfloat16 [512, 2048], P(('dp', 'ctx', 'tp'))
- grad_w_gate: bfloat16 [64, 2048, 1536], P(('dp', 'ctx'), None, 'tp')
- grad_w_up: bfloat16 [64, 2048, 1536], P(('dp', 'ctx'), None, 'tp')
- grad_w_down: bfloat16 [64, 1536, 2048], P(('dp', 'ctx'), 'tp')
Inputs may be any that keep to these rules, and one draw needn't show every extreme that they name: `expert_ids`: each row names 8 different experts. Among the tokens of one index of dp and ctx no expert is named by more than 16 of them, and in every draw some expert is named by exactly 16 of them.
All inputs are finite; a program needn't handle non-finite values.
Results may differ from a plain program's by a relative error of at most 0.012.
Values may be sent and summed in bfloat16 or wider, within the bound.
A program may use at most 384 MiB of HBM per device.

v0:
```python
import jax
import jax.numpy as jnp
from jax import lax
from jax.experimental import pallas as pl
from jax.experimental.pallas import tpu as pltpu
from jax.sharding import PartitionSpec as P

contract_last = (((1,), (1,)), ((), ()))
contract_first = (((0,), (0,)), ((), ()))


def swiglu_rows(inputs, cotangent, row_weights, gate_w, up_w, down_w):
    gate = jnp.dot(inputs, gate_w, preferred_element_type=jnp.float32)
    upward = jnp.dot(inputs, up_w, preferred_element_type=jnp.float32)
    sigmoid_gate = jax.nn.sigmoid(gate)
    row_scale = row_weights.astype(jnp.float32)[:, None]
    activation = (row_scale * gate * sigmoid_gate * upward).astype(jnp.bfloat16)
    output_rows = jnp.dot(activation, down_w, preferred_element_type=jnp.float32).astype(
        jnp.bfloat16
    )
    backward = lax.dot_general(cotangent, down_w, contract_last, preferred_element_type=jnp.float32)
    grad_gate_pre = (
        backward * row_scale * upward * sigmoid_gate * (1.0 + gate * (1.0 - sigmoid_gate))
    ).astype(jnp.bfloat16)
    grad_up_pre = (backward * row_scale * gate * sigmoid_gate).astype(jnp.bfloat16)
    input_rows = (
        lax.dot_general(grad_gate_pre, gate_w, contract_last, preferred_element_type=jnp.float32)
        + lax.dot_general(grad_up_pre, up_w, contract_last, preferred_element_type=jnp.float32)
    ).astype(jnp.bfloat16)
    grad_down = lax.dot_general(
        activation, cotangent, contract_first, preferred_element_type=jnp.float32
    )
    grad_gate = lax.dot_general(
        inputs, grad_gate_pre, contract_first, preferred_element_type=jnp.float32
    )
    grad_up = lax.dot_general(
        inputs, grad_up_pre, contract_first, preferred_element_type=jnp.float32
    )
    return (output_rows, input_rows, grad_gate, grad_up, grad_down)


def shards(tokens, grad_out, expert_ids, router_weights, w_gate, w_up, w_down):
    expert_devices = lax.axis_size(("dp", "ctx"))
    group_rows, top_count = expert_ids.shape
    local_experts = w_gate.shape[0]
    expert_total = expert_devices * local_experts
    slot_most = 2 * group_rows * top_count // expert_total
    model_width = tokens.shape[1]
    group_tokens, group_grads = (
        lax.all_to_all(tokens, "tp", split_axis=1, concat_axis=0, tiled=True),
        lax.all_to_all(grad_out, "tp", split_axis=1, concat_axis=0, tiled=True),
    )
    carried = group_tokens.shape[1]
    flat_ids = expert_ids.reshape(-1)
    onehot = (flat_ids[:, None] == jnp.arange(expert_total, dtype=jnp.int32)[None, :]).astype(
        jnp.int32
    )
    earlier = jnp.cumsum(onehot, axis=0) - onehot
    ranks = jnp.sum(earlier * onehot, axis=1)
    slots = flat_ids * slot_most + ranks
    assignments = group_rows * top_count
    source = (
        jnp.full((expert_total * slot_most,), assignments, jnp.int32)
        .at[slots]
        .set(jnp.arange(assignments, dtype=jnp.int32))
    )
    token_of = source // top_count
    zero_row = jnp.zeros((1, carried), jnp.bfloat16)
    send_tokens = jnp.concatenate([group_tokens, zero_row], axis=0)[token_of].reshape(
        expert_devices, local_experts * slot_most, carried
    )
    send_grads = jnp.concatenate([group_grads, zero_row], axis=0)[token_of].reshape(
        expert_devices, local_experts * slot_most, carried
    )
    send_weights = jnp.concatenate(
        [router_weights.reshape(-1), jnp.zeros((1,), jnp.bfloat16)], axis=0
    )[source].reshape(expert_devices, local_experts * slot_most)
    recv_tokens, recv_grads, recv_weights = (
        lax.all_to_all(send_tokens, ("dp", "ctx"), split_axis=0, concat_axis=0, tiled=True),
        lax.all_to_all(send_grads, ("dp", "ctx"), split_axis=0, concat_axis=0, tiled=True),
        lax.all_to_all(send_weights, ("dp", "ctx"), split_axis=0, concat_axis=0, tiled=True),
    )
    recv_tokens, recv_grads = (
        lax.all_gather(recv_tokens, "tp", axis=2, tiled=True),
        lax.all_gather(recv_grads, "tp", axis=2, tiled=True),
    )
    token_grid = recv_tokens.reshape(expert_devices, local_experts, slot_most, model_width)
    grad_grid = recv_grads.reshape(expert_devices, local_experts, slot_most, model_width)
    weight_grid = recv_weights.reshape(expert_devices, local_experts, slot_most)
    outputs = []
    for expert_index in range(local_experts):
        outputs.append(
            swiglu_rows(
                token_grid[:, expert_index].reshape(-1, model_width),
                grad_grid[:, expert_index].reshape(-1, model_width),
                weight_grid[:, expert_index].reshape(-1),
                w_gate[expert_index],
                w_up[expert_index],
                w_down[expert_index],
            )
        )
    out_rows = jnp.stack(
        [entry[0].reshape(expert_devices, slot_most, model_width) for entry in outputs], axis=1
    ).reshape(expert_devices, local_experts * slot_most, model_width)
    in_rows = jnp.stack(
        [entry[1].reshape(expert_devices, slot_most, model_width) for entry in outputs], axis=1
    ).reshape(expert_devices, local_experts * slot_most, model_width)
    grad_gate = jnp.stack([entry[2] for entry in outputs], axis=0).astype(jnp.bfloat16)
    grad_up = jnp.stack([entry[3] for entry in outputs], axis=0).astype(jnp.bfloat16)
    grad_down = jnp.stack([entry[4] for entry in outputs], axis=0).astype(jnp.bfloat16)
    slot_grid = slots.reshape(group_rows, top_count)

    def combine(table):
        picked = table.reshape(expert_total * slot_most, -1)[slot_grid]
        return jnp.sum(picked, axis=1)

    column_out, column_in = (
        lax.psum_scatter(
            out_rows.astype(jnp.float32).astype(jnp.bfloat16), "tp", scatter_dimension=2, tiled=True
        ).astype(jnp.float32),
        lax.psum_scatter(
            in_rows.astype(jnp.float32).astype(jnp.bfloat16), "tp", scatter_dimension=2, tiled=True
        ).astype(jnp.float32),
    )
    back_out, back_in = (
        lax.all_to_all(
            column_out.astype(jnp.bfloat16), ("dp", "ctx"), split_axis=0, concat_axis=0, tiled=True
        ).astype(column_out.dtype),
        lax.all_to_all(
            column_in.astype(jnp.bfloat16), ("dp", "ctx"), split_axis=0, concat_axis=0, tiled=True
        ).astype(column_in.dtype),
    )
    layer_out, grad_tokens = (
        lax.all_to_all(
            combine(back_out).astype(jnp.bfloat16), "tp", split_axis=0, concat_axis=1, tiled=True
        ).astype(jnp.float32),
        lax.all_to_all(
            combine(back_in).astype(jnp.bfloat16), "tp", split_axis=0, concat_axis=1, tiled=True
        ).astype(jnp.float32),
    )
    return (
        layer_out.astype(jnp.bfloat16),
        grad_tokens.astype(jnp.bfloat16),
        grad_gate,
        grad_up,
        grad_down,
    )


def select_rows(order, row_count):
    rows = lax.broadcasted_iota(jnp.int32, (row_count, order.shape[-1]), 0)
    return rows == order


def rows_kernel(
    tokens, grads, order_row, scale_row, order_col, gate_w, up_w, down_w,
    inputs_out, cotangent_out, act_out, gate_pre_out, up_pre_out, sums_out,
    out_rows, in_rows,
):
    f32, bf16 = jnp.float32, jnp.bfloat16
    expert = pl.program_id(0)
    expert_count = order_col.shape[1]
    row_count = inputs_out.shape[1]
    token_count, width = tokens.shape
    picked = select_rows(order_row[0], row_count)
    row_scale = jnp.sum(jnp.where(picked, scale_row[0], 0.0), axis=1, keepdims=True)
    pick = jnp.where(picked, 1.0, 0.0).astype(bf16)
    inputs = jnp.dot(pick, tokens[...], preferred_element_type=f32).astype(bf16)
    cotangent = jnp.dot(pick, grads[...], preferred_element_type=f32).astype(bf16)
    inputs_out[0] = inputs
    cotangent_out[0] = cotangent
    gate = jnp.dot(inputs, gate_w[0], preferred_element_type=f32)
    upward = jnp.dot(inputs, up_w[0], preferred_element_type=f32)
    backward = lax.dot_general(cotangent, down_w[0], contract_last, preferred_element_type=f32)
    sigmoid_gate = jax.nn.sigmoid(gate)
    silu = row_scale * gate * sigmoid_gate
    act = (silu * upward).astype(bf16)
    gate_pre = (
        backward * row_scale * upward * sigmoid_gate * (1.0 + gate * (1.0 - sigmoid_gate))
    ).astype(bf16)
    up_pre = (backward * silu).astype(bf16)
    act_out[0] = act
    gate_pre_out[0] = gate_pre
    up_pre_out[0] = up_pre
    here = pl.ds(pl.multiple_of(expert * row_count, row_count), row_count)
    out_rows[here, :] = jnp.dot(act, down_w[0], preferred_element_type=f32).astype(bf16)
    in_rows[here, :] = (
        lax.dot_general(gate_pre, gate_w[0], contract_last, preferred_element_type=f32)
        + lax.dot_general(up_pre, up_w[0], contract_last, preferred_element_type=f32)
    ).astype(bf16)

    @pl.when(expert == expert_count - 1)
    def _():
        lanes = lax.broadcasted_iota(jnp.int32, (token_count, row_count), 1)
        place = jnp.concatenate(
            [
                jnp.where(lanes == order_col[:, e : e + 1], 1.0, 0.0).astype(bf16)
                for e in range(expert_count)
            ],
            axis=1,
        )
        sums_out[:, :width] = jnp.dot(
            place, out_rows[...], preferred_element_type=f32
        ).astype(bf16)
        sums_out[:, width:] = jnp.dot(
            place, in_rows[...], preferred_element_type=f32
        ).astype(bf16)


def weights_kernel(inputs, cotangent, act, gate_pre, up_pre, gate_out, up_out, down_out):
    f32, bf16 = jnp.float32, jnp.bfloat16
    gate_out[0] = lax.dot_general(
        inputs[0], gate_pre[0], contract_first, preferred_element_type=f32
    ).astype(bf16)
    up_out[0] = lax.dot_general(
        inputs[0], up_pre[0], contract_first, preferred_element_type=f32
    ).astype(bf16)
    down_out[0] = lax.dot_general(
        act[0], cotangent[0], contract_first, preferred_element_type=f32
    ).astype(bf16)


def gathered_shards(tokens, grad_out, expert_ids, router_weights, w_gate, w_up, w_down):
    f32, bf16, i32 = jnp.float32, jnp.bfloat16, jnp.int32
    axes = ("dp", "ctx", "tp")
    own_tokens, width = tokens.shape
    group_rows, top_count = expert_ids.shape
    experts, _, hidden = w_gate.shape
    groups = lax.axis_size(("dp", "ctx"))
    row_count = groups * (2 * group_rows * top_count // (groups * experts))
    start = lax.axis_index("tp") * own_tokens
    own_ids = lax.dynamic_slice_in_dim(expert_ids, start, own_tokens, 0)
    own_weights = lax.dynamic_slice_in_dim(router_weights, start, own_tokens, 0)
    routing = jnp.concatenate(
        [own_ids.astype(bf16), own_weights, jnp.zeros((own_tokens, 128 - 2 * top_count), bf16)],
        axis=1,
    )
    carried = lax.all_gather(
        jnp.concatenate([tokens, grad_out, routing], axis=1), axes, axis=0, tiled=True
    )
    total = carried.shape[0]
    ids = carried[:, 2 * width : 2 * width + top_count].astype(i32)
    weights = carried[:, 2 * width + top_count : 2 * width + 2 * top_count].astype(f32)
    first = lax.axis_index(("dp", "ctx")) * experts
    named = ids[:, None, :] == (first + jnp.arange(experts, dtype=i32))[None, :, None]
    scale = jnp.sum(jnp.where(named, weights[:, None, :], 0.0), axis=2)
    hit = jnp.any(named, axis=2)
    place = jnp.arange(total, dtype=i32)
    earlier = (place[:, None] > place[None, :]).astype(bf16)
    rank = jnp.dot(earlier, hit.astype(bf16), preferred_element_type=f32).astype(i32)
    order_col = jnp.where(hit, rank, -1)
    order_row = order_col.T.reshape(experts, 1, total)
    scale_row = scale.T.reshape(experts, 1, total)

    whole = lambda shape, column=0: pl.BlockSpec(shape, lambda e: (0, column))
    each = lambda *shape: pl.BlockSpec((1, *shape), lambda e: (e, 0, 0))
    rows_shape = lambda n: jax.ShapeDtypeStruct((experts, row_count, n), bf16)
    matmul = 2 * experts * row_count * width * hidden
    inputs, cotangent, act, gate_pre, up_pre, sums = pl.pallas_call(
        rows_kernel,
        grid=(experts,),
        in_specs=[
            whole((total, width)),
            whole((total, width), 1),
            each(1, total),
            each(1, total),
            whole((total, experts)),
            each(width, hidden),
            each(width, hidden),
            each(hidden, width),
        ],
        out_specs=[
            each(row_count, width),
            each(row_count, width),
            each(row_count, hidden),
            each(row_count, hidden),
            each(row_count, hidden),
            whole((total, 2 * width)),
        ],
        out_shape=[
            rows_shape(width),
            rows_shape(width),
            rows_shape(hidden),
            rows_shape(hidden),
            rows_shape(hidden),
            jax.ShapeDtypeStruct((total, 2 * width), bf16),
        ],
        scratch_shapes=[
            pltpu.VMEM((experts * row_count, width), bf16),
            pltpu.VMEM((experts * row_count, width), bf16),
        ],
        compiler_params=pltpu.CompilerParams(vmem_limit_bytes=60 << 20),
        cost_estimate=pl.CostEstimate(
            flops=6 * matmul, bytes_accessed=6 * experts * width * hidden, transcendentals=0
        ),
        name="expert_rows",
    )(carried, carried, order_row, scale_row, order_col, w_gate, w_up, w_down)
    summed = lax.psum_scatter(sums, axes, scatter_dimension=0, tiled=True)
    grad_gate, grad_up, grad_down = pl.pallas_call(
        weights_kernel,
        grid=(experts,),
        in_specs=[
            each(row_count, width),
            each(row_count, width),
            each(row_count, hidden),
            each(row_count, hidden),
            each(row_count, hidden),
        ],
        out_specs=[each(width, hidden), each(width, hidden), each(hidden, width)],
        out_shape=[
            jax.ShapeDtypeStruct(w_gate.shape, bf16),
            jax.ShapeDtypeStruct(w_up.shape, bf16),
            jax.ShapeDtypeStruct(w_down.shape, bf16),
        ],
        compiler_params=pltpu.CompilerParams(vmem_limit_bytes=60 << 20),
        cost_estimate=pl.CostEstimate(
            flops=3 * matmul, bytes_accessed=6 * experts * width * hidden, transcendentals=0
        ),
        name="expert_weights",
    )(inputs, cotangent, act, gate_pre, up_pre)
    return summed[:, :width], summed[:, width:], grad_gate, grad_up, grad_down


def solution(mesh):
    def per_device(tokens, *rest):
        devices = lax.axis_size(("dp", "ctx", "tp"))
        few = tokens.shape[0] * devices <= 1024
        return (gathered_shards if few else shards)(tokens, *rest)

    placed = (
        P(("dp", "ctx", "tp"), None),
        P(("dp", "ctx", "tp"), None),
        P(("dp", "ctx"), None),
        P(("dp", "ctx"), None),
        P(("dp", "ctx"), None, "tp"),
        P(("dp", "ctx"), None, "tp"),
        P(("dp", "ctx"), "tp", None),
    )
    return jax.shard_map(
        per_device,
        mesh=mesh,
        in_specs=placed,
        out_specs=(
            P(("dp", "ctx", "tp"), None),
            P(("dp", "ctx", "tp"), None),
            P(("dp", "ctx"), None, "tp"),
            P(("dp", "ctx"), None, "tp"),
            P(("dp", "ctx"), "tp", None),
        ),
        check_vma=False,
    )
```

profile of v0, /device:TPU:0, one launch (start us, length us, event | category | flops | bytes accessed | tf_op | source)
XLA Modules:
  0.0 263.6 jit_solution(12499478694188588543)
XLA Ops:
  7.2 0.0 copy-start
  7.2 0.0 all-gather.2.cloned.1.call-start
  7.2 0.8 constant_dynamic-slice_fusion
  8.0 0.1 copy.32
  8.1 0.0 copy-done
  8.1 0.1 constant_dynamic-slice_fusion.1
  8.2 0.1 copy.31
  8.2 1.6 concatenate.3
  9.9 0.0 all-gather.2.cloned.1.call-update
  9.9 0.0 reduce-scatter.2.cloned.1.call-start
  9.9 66.8 %all-gather.2.cloned.1.call-done.tokens.grads = bf16[512,4224]{1,0:T(8,128)(2,1)} async-done(((bf16[16,4224]{1,0:T(8,128)(2,1)}), bf16[512,4224]{1,0:T(8,128)(2,1)}) %all-gather.2.cloned.1.call-update) | async-done | bytes 4325392 | tf_op jit(solution)/shard_map/all_gather | solution.py:238
  76.8 1.1 slice_convert_fusion
  77.9 0.1 copy.28
  78.0 0.1 copy.25
  78.1 0.1 compare_reduce_fusion
  78.2 0.1 fusion.1
  78.3 0.6 reshape.23.scale_row
  78.9 0.2 copy.27
  79.1 0.3 fusion.order_col
  79.4 0.0 copy-start.2
  79.4 0.7 copy.29.order_row
  80.1 0.0 copy-done.2
  80.1 0.0 copy-start.1
  80.1 35.6 %expert_rows.1 = (bf16[8,128,2048]{2,1,0:T(8,128)(2,1)}, bf16[8,128,2048]{2,1,0:T(8,128)(2,1)}, bf16[8,128,384]{2,1,0:T(8,128)(2,1)}, bf16[8,128,384]{2,1,0:T(8,...) custom-call(bf16[512,4224]{1,0:T(8,128)(2,1)} %all-gather.2.cloned.1.call-done.tokens.grads, ...), custom_call_target="tpu_custom_call" | custom-call | flops 9663676416 | bytes 37748736 | tf_op jit(solution)/shard_map/expert_rows/pallas_call | solution.py:259
  115.7 0.0 reduce-scatter.2.cloned.1.call-update
  115.8 17.6 %expert_weights.1 = (bf16[8,2048,384]{2,1,0:T(8,128)(2,1)}, bf16[8,2048,384]{2,1,0:T(8,128)(2,1)}, bf16[8,384,2048]{2,1,0:T(8,128)(2,1)}) custom-call(bf16[8,128,2048]{2,1,0:T(8,128)(2,1)} %get-tuple-element.15.inputs, bf16[8,128,2048]{2,1,0:T(8,128)(2,1)} %get-tuple-element.16.cotangent, bf16[8,128,384]{2,1,0:T(8,128)(2,1)} %get-tuple-element.17.act, ...), custom_call_target="tpu_custom_call" | custom-call | flops 4831838208 | bytes 37748736 | tf_op jit(solution)/shard_map/expert_weights/pallas_call | solution.py:299
  133.3 121.9 %reduce-scatter.2.cloned.1.call-done = bf16[16,4096]{1,0:T(8,128)(2,1)} async-done(((bf16[512,4096]{1,0:T(8,128)(2,1)}), bf16[16,4096]{1,0:T(8,128)(2,1)}) %reduce-scatter.2.cloned.1.call-update) | async-done | bytes 131088 | tf_op jit(solution)/shard_map/reduce_scatter | solution.py:298
  255.3 1.5 fusion.2
  256.8 0.0 copy-done.1
  (3 shorter events, 0.0 us)
Async XLA Ops:
  7.2 0.9 copy-start
  7.2 69.6 %all-gather.2.cloned.1.call-start = ((), (), s32[]{:S(2)}) async-start(), calls=%async_computation.1 | async-start | bytes 4460544 | tf_op jit(solution)/shard_map/all_gather | solution.py:238
  9.9 245.4 %reduce-scatter.2.cloned.1.call-start = ((), (), s32[]{:S(2)}) async-start(), calls=%async_computation.2 | async-start | bytes 4325376 | tf_op jit(solution)/shard_map/reduce_scatter | solution.py:298
  79.4 0.7 copy-start.2
  80.1 176.7 %copy-start.1 = (s32[64,8]{0,1:T(8,128)S(1)}, s32[64,8]{0,1:T(8,128)}, u32[]{:S(2)}) copy-start(s32[64,8]{0,1:T(8,128)} %param.9) | copy-start | bytes 6148
Sparse Core Ops, SparseCore 0:
  11.5 65.2 all-gather.1
  115.9 139.3 reduce-scatter.1
where the time goes:
time: 264 us
  waiting for transfers between devices  189 us (72%)
  Pallas kernels  53.2 us (20%)
  between operations  14.1 us (5%)
  local copies, waits for them, and re-layouts  5.84 us (2%)
    reduce_scatter x1, waiting for transfers between devices, gathered_shards(): summed = lax.psum_scatter(sums, axes, scatter_dimension=0, tiled=True)  122 us
    all_gather x1, waiting for transfers between devices, gathered_shards(): lax.all_gather(jnp.concatenate([tokens, grad_out, routing], axis=1), axes...  66.8 us
    pallas_call x1, Pallas kernels, gathered_shards(): pl.pallas_call(rows_kernel, grid=(experts,), in_specs=[whole((total, widt...  35.6 us
    pallas_call x1, Pallas kernels, gathered_shards(): pl.pallas_call(weights_kernel, grid=(experts,), in_specs=[each(row_count,...  17.6 us
  transfers between devices with their start and end apart: 2, of which 2 were waited for; matrix products, arithmetic and copies ran while one was open for 0% of the time, Pallas kernels for 7%

commit v1 on v0

--- a/solution.py
+++ b/solution.py
@@ -150,6 +150,183 @@
 def select_rows(order, row_count):
     rows = lax.broadcasted_iota(jnp.int32, (row_count, order.shape[-1]), 0)
     return rows == order
+
+
+class Place:
+    def __init__(self):
+        self.ring = lax.axis_size("dp")
+        self.z, self.x = lax.axis_index("dp"), lax.axis_index("ctx")
+        tp = lax.axis_index("tp")
+        self.y, self.c = tp // 2, tp % 2
+
+    def device(self, z=None, x=None, y=None, c=None):
+        pick = lambda value, own: own if value is None else value
+        tp = pick(y, self.y) * 2 + pick(c, self.c)
+        return (pick(z, self.z), pick(x, self.x), tp)
+
+    def meet(self):
+        barrier = pltpu.get_barrier_semaphore()
+        others = [self.core_peer(), self.x_peer(), self.y_peer()]
+        others += [self.device(z=lax.rem(self.z + k, self.ring)) for k in range(1, self.ring)]
+        for other in others:
+            pl.semaphore_signal(
+                barrier, inc=1, device_id=other, device_id_type=pl.DeviceIdType.MESH
+            )
+        pl.semaphore_wait(barrier, len(others))
+
+    def core_peer(self):
+        return self.device(c=1 - self.c)
+
+    def x_peer(self):
+        return self.device(x=1 - self.x)
+
+    def y_peer(self):
+        return self.device(y=1 - self.y)
+
+
+def start_send(source, target, send_sem, recv_sem, device):
+    copy = pltpu.make_async_remote_copy(
+        src_ref=source,
+        dst_ref=target,
+        send_sem=send_sem,
+        recv_sem=recv_sem,
+        device_id=device,
+        device_id_type=pl.DeviceIdType.MESH,
+    )
+    copy.start()
+    return copy
+
+
+def gather_kernel(own_a, own_b, all_a, all_b, send_sems, recv_sems, local_sems):
+    at = Place()
+    z, x, y, c, ring = at.z, at.x, at.y, at.c, at.ring
+    own, full = (own_a, own_b), (all_a, all_b)
+    stay = []
+    for h in range(2):
+        copy = pltpu.make_async_copy(own[h], full[h].at[z, x, y, c], local_sems.at[h])
+        copy.start()
+        stay.append(copy)
+    at.meet()
+    sems = lambda stage, h, k: (send_sems.at[stage, h, k], recv_sems.at[stage, h, k])
+    first, second, third, along = {}, {}, {}, {}
+    peers = ((at.x_peer(), at.y_peer()), (at.y_peer(), at.x_peer()))
+    for h in range(2):
+        here = full[h].at[z, x, y, c]
+        first[h, 0] = start_send(own[h], here, *sems(1, h, 0), peers[h][0])
+        for k in range(1, ring):
+            away = at.device(z=lax.rem(z + k, ring))
+            along[h, k] = start_send(own[h], here, *sems(0, h, k), away)
+    for copy in stay:
+        copy.wait()
+    for k in range(ring):
+        zz = lax.rem(z - k + ring, ring)
+        for h in range(2):
+            if k > 0:
+                along[h, k].wait_recv()
+                block = full[h].at[zz, x, y, c]
+                first[h, k] = start_send(block, block, *sems(1, h, k), peers[h][0])
+    for k in range(ring):
+        zz = lax.rem(z - k + ring, ring)
+        for h in range(2):
+            first[h, k].wait_recv()
+            block = full[h].at[zz, :, y, c] if h == 0 else full[h].at[zz, x, :, c]
+            second[h, k] = start_send(block, block, *sems(2, h, k), peers[h][1])
+    for k in range(ring):
+        zz = lax.rem(z - k + ring, ring)
+        for h in range(2):
+            second[h, k].wait_recv()
+            block = full[h].at[zz, :, :, c]
+            third[h, k] = start_send(block, block, *sems(3, h, k), at.core_peer())
+    for copy in third.values():
+        copy.wait_recv()
+    for copies in (along, first, second, third):
+        for copy in copies.values():
+            copy.wait_send()
+
+
+def gather_all(own_a, own_b):
+    ring = lax.axis_size("dp")
+    full = lambda own: jax.ShapeDtypeStruct((ring, 2, 2, 2, *own.shape), own.dtype)
+    anywhere = pl.BlockSpec(memory_space=pl.ANY)
+    return pl.pallas_call(
+        gather_kernel,
+        in_specs=[anywhere, anywhere],
+        out_specs=[anywhere, anywhere],
+        out_shape=[full(own_a), full(own_b)],
+        scratch_shapes=[
+            pltpu.SemaphoreType.DMA((4, 2, ring)),
+            pltpu.SemaphoreType.DMA((4, 2, ring)),
+            pltpu.SemaphoreType.DMA((2,)),
+        ],
+        compiler_params=pltpu.CompilerParams(collective_id=0, has_side_effects=True),
+        name="gather_all",
+    )(own_a, own_b)
+
+
+def reduce_kernel(sums, out_a, out_b, got1, sum1, got2, sum2, got3, sum3, got4, send_sems, recv_sems):
+    at = Place()
+    z, x, y, c, ring = at.z, at.x, at.y, at.c, at.ring
+    f32, bf16 = jnp.float32, jnp.bfloat16
+    at.meet()
+    sems = lambda stage, h, k: (send_sems.at[stage, h, k], recv_sems.at[stage, h, k])
+    peers = ((at.y_peer(), at.x_peer()), (at.x_peer(), at.y_peer()))
+    copies = [{}, {}, {}, {}]
+    pairs = [(k, h) for k in range(ring) for h in range(2)]
+    aim = [lax.rem(z + 1 + k, ring) for k in range(ring)]
+    for k, h in pairs:
+        copies[0][h, k] = start_send(
+            sums.at[h, aim[k], :, :, 1 - c], got1.at[h, k], *sems(0, h, k), at.core_peer()
+        )
+    for k, h in pairs:
+        copies[0][h, k].wait_recv()
+        sum1[h, k] = (sums[h, aim[k], :, :, c].astype(f32) + got1[h, k].astype(f32)).astype(bf16)
+        part = sum1.at[h, k, :, 1 - y] if h == 0 else sum1.at[h, k, 1 - x]
+        copies[1][h, k] = start_send(part, got2.at[h, k], *sems(1, h, k), peers[h][0])
+    for k, h in pairs:
+        copies[1][h, k].wait_recv()
+        mine = sum1[h, k, :, y] if h == 0 else sum1[h, k, x]
+        sum2[h, k] = (mine.astype(f32) + got2[h, k].astype(f32)).astype(bf16)
+        part = sum2.at[h, k, 1 - x] if h == 0 else sum2.at[h, k, 1 - y]
+        copies[2][h, k] = start_send(part, got3.at[h, k], *sems(2, h, k), peers[h][1])
+    for k, h in pairs:
+        copies[2][h, k].wait_recv()
+        mine = sum2[h, k, x] if h == 0 else sum2[h, k, y]
+        sum3[h, k] = (mine.astype(f32) + got3[h, k].astype(f32)).astype(bf16)
+        if k < ring - 1:
+            copies[3][h, k] = start_send(
+                sum3.at[h, k], got4.at[h, k], *sems(3, h, k), at.device(z=aim[k])
+            )
+    for h, out in enumerate((out_a, out_b)):
+        total = sum3[h, ring - 1].astype(f32)
+        for k in range(ring - 1):
+            copies[3][h, k].wait_recv()
+            total = total + got4[h, k].astype(f32)
+        out[...] = total.astype(bf16)
+    for stage in copies:
+        for copy in stage.values():
+            copy.wait_send()
+
+
+def reduce_all(sums):
+    _, ring, _, _, _, rows, width = sums.shape
+    out = jax.ShapeDtypeStruct((rows, width), sums.dtype)
+    in_vmem = pl.BlockSpec(memory_space=pltpu.VMEM)
+    table = lambda *lead: pltpu.VMEM((2, ring, *lead, rows, width), sums.dtype)
+    return pl.pallas_call(
+        reduce_kernel,
+        in_specs=[in_vmem],
+        out_specs=[in_vmem, in_vmem],
+        out_shape=[out, out],
+        scratch_shapes=[
+            table(2, 2), table(2, 2), table(2), table(2), table(), table(), table(),
+            pltpu.SemaphoreType.DMA((4, 2, ring)),
+            pltpu.SemaphoreType.DMA((4, 2, ring)),
+        ],
+        compiler_params=pltpu.CompilerParams(
+            collective_id=1, has_side_effects=True, vmem_limit_bytes=40 << 20
+        ),
+        name="reduce_all",
+    )(sums)
 
 
 def rows_kernel(
@@ -199,10 +376,10 @@
             ],
             axis=1,
         )
-        sums_out[:, :width] = jnp.dot(
+        sums_out[0] = jnp.dot(
             place, out_rows[...], preferred_element_type=f32
         ).astype(bf16)
-        sums_out[:, width:] = jnp.dot(
+        sums_out[1] = jnp.dot(
             place, in_rows[...], preferred_element_type=f32
         ).astype(bf16)
 
@@ -222,7 +399,6 @@
 
 def gathered_shards(tokens, grad_out, expert_ids, router_weights, w_gate, w_up, w_down):
     f32, bf16, i32 = jnp.float32, jnp.bfloat16, jnp.int32
-    axes = ("dp", "ctx", "tp")
     own_tokens, width = tokens.shape
     group_rows, top_count = expert_ids.shape
     experts, _, hidden = w_gate.shape
@@ -235,12 +411,11 @@
         [own_ids.astype(bf16), own_weights, jnp.zeros((own_tokens, 128 - 2 * top_count), bf16)],
         axis=1,
     )
-    carried = lax.all_gather(
-        jnp.concatenate([tokens, grad_out, routing], axis=1), axes, axis=0, tiled=True
-    )
+    all_tokens, carried = gather_all(tokens, jnp.concatenate([grad_out, routing], axis=1))
+    all_tokens, carried = all_tokens.reshape(-1, width), carried.reshape(-1, width + 128)
     total = carried.shape[0]
-    ids = carried[:, 2 * width : 2 * width + top_count].astype(i32)
-    weights = carried[:, 2 * width + top_count : 2 * width + 2 * top_count].astype(f32)
+    ids = carried[:, width : width + top_count].astype(i32)
+    weights = carried[:, width + top_count : width + 2 * top_count].astype(f32)
     first = lax.axis_index(("dp", "ctx")) * experts
     named = ids[:, None, :] == (first + jnp.arange(experts, dtype=i32))[None, :, None]
     scale = jnp.sum(jnp.where(named, weights[:, None, :], 0.0), axis=2)
@@ -252,7 +427,7 @@
     order_row = order_col.T.reshape(experts, 1, total)
     scale_row = scale.T.reshape(experts, 1, total)
 
-    whole = lambda shape, column=0: pl.BlockSpec(shape, lambda e: (0, column))
+    whole = lambda *shape: pl.BlockSpec(shape, lambda e: (0,) * len(shape))
     each = lambda *shape: pl.BlockSpec((1, *shape), lambda e: (e, 0, 0))
     rows_shape = lambda n: jax.ShapeDtypeStruct((experts, row_count, n), bf16)
     matmul = 2 * experts * row_count * width * hidden
@@ -260,11 +435,11 @@
         rows_kernel,
         grid=(experts,),
         in_specs=[
-            whole((total, width)),
-            whole((total, width), 1),
+            whole(total, width),
+            whole(total, width),
             each(1, total),
             each(1, total),
-            whole((total, experts)),
+            whole(total, experts),
             each(width, hidden),
             each(width, hidden),
             each(hidden, width),
@@ -275,7 +450,7 @@
             each(row_count, hidden),
             each(row_count, hidden),
             each(row_count, hidden),
-            whole((total, 2 * width)),
+            whole(2, total, width),
         ],
         out_shape=[
             rows_shape(width),
@@ -283,7 +458,7 @@
             rows_shape(hidden),
             rows_shape(hidden),
             rows_shape(hidden),
-            jax.ShapeDtypeStruct((total, 2 * width), bf16),
+            jax.ShapeDtypeStruct((2, total, width), bf16),
         ],
         scratch_shapes=[
             pltpu.VMEM((experts * row_count, width), bf16),
@@ -294,8 +469,10 @@
             flops=6 * matmul, bytes_accessed=6 * experts * width * hidden, transcendentals=0
         ),
         name="expert_rows",
-    )(carried, carried, order_row, scale_row, order_col, w_gate, w_up, w_down)
-    summed = lax.psum_scatter(sums, axes, scatter_dimension=0, tiled=True)
+    )(all_tokens, carried, order_row, scale_row, order_col, w_gate, w_up, w_down)
+    layer_out, grad_tokens = reduce_all(
+        sums.reshape(2, lax.axis_size("dp"), 2, 2, 2, own_tokens, width)
+    )
     grad_gate, grad_up, grad_down = pl.pallas_call(
         weights_kernel,
         grid=(experts,),
@@ -318,13 +495,14 @@
         ),
         name="expert_weights",
     )(inputs, cotangent, act, gate_pre, up_pre)
-    return summed[:, :width], summed[:, width:], grad_gate, grad_up, grad_down
+    return layer_out, grad_tokens, grad_gate, grad_up, grad_down
 
 
 def solution(mesh):
     def per_device(tokens, *rest):
         devices = lax.axis_size(("dp", "ctx", "tp"))
         few = tokens.shape[0] * devices <= 1024
+        few = few and lax.axis_size("ctx") == 2 and lax.axis_size("tp") == 4
         return (gathered_shards if few else shards)(tokens, *rest)
 
     placed = (

time: 264 us -> 130 us (0.49)
  waiting for transfers between devices: 189 us -> 0 us
  Pallas kernels: 53.2 us -> 119 us
  between operations: 14.1 us -> 0.73 us
    reduce_scatter x1 -> x0, waiting for transfers between devices: 122 us -> none  [gathered_shards(): summed = lax.psum_scatter(sums, axes, scatter_dimension=0, tiled=True)]
    all_gather x1 -> x0, waiting for transfers between devices: 66.8 us -> none  [gathered_shards(): lax.all_gather(jnp.concatenate([tokens, grad_out, routing], axis=1), axes...]
    pallas_call x1 -> x3, Pallas kernels: 35.6 us -> 102 us  [the longest x1 35.6 us: gathered_shards(): pl.pallas_call(rows_kernel, grid=(experts,), in_specs=[whole(total, width...]
    unnamed x8 -> x12, local copies, waits for them, and re-layouts: 0.18 us -> 3.62 us
  transfers between devices with their start and end apart: 2 -> 0, of which waited for: 2 -> 0; matrix products, arithmetic and copies ran while one was open for 0% -> 0% of each run, Pallas kernels for 7% -> 0%
where the time goes in v1:
time: 130 us
  Pallas kernels  119 us (92%)
  local copies, waits for them, and re-layouts  7.7 us (6%)
  other arithmetic  1.34 us (1%)
    pallas_call x1, Pallas kernels, gathered_shards(): pl.pallas_call(rows_kernel, grid=(experts,), in_specs=[whole(total, width...  35.6 us
    pallas_call x1, Pallas kernels, gather_all(): pl.pallas_call(gather_kernel, in_specs=[anywhere, anywhere], out_specs=[a...  35 us
    pallas_call x1, Pallas kernels, reduce_all(): pl.pallas_call(reduce_kernel, in_specs=[in_vmem], out_specs=[in_vmem, in_...  31.4 us
    pallas_call x1, Pallas kernels, gathered_shards(): pl.pallas_call(weights_kernel, grid=(experts,), in_specs=[each(row_count,...  17.5 us
    unnamed x12, local copies, waits for them, and re-layouts  3.62 us

profile of v1, /device:TPU:0, one launch (start us, length us, event | category | flops | bytes accessed | tf_op | source)
XLA Modules:
  0.0 129.5 jit_solution(14266616066406424667)
XLA Ops:
  0.6 0.0 copy-start
  0.7 0.8 constant_dynamic-slice_fusion
  1.4 0.1 copy.32
  1.5 0.0 copy-done
  1.5 0.1 constant_dynamic-slice_fusion.1
  1.6 0.1 copy.31
  1.7 1.6 %concatenate.3.own_b = bf16[16,2176]{1,0:T(8,128)(2,1)} concatenate(bf16[16,2048]{1,0:T(8,128)(2,1)} %param.8, bf16[16,8]{1,0:T(8,128)(2,1)S(1)} %convert_element_type.16, bf16[16,8]{1,0:T(8,128)(2,1)S(1)} %copy.32, bf16[16,112]{1,0:T(8,128)(2,1)S(1)} %broadcast_in_dim.24), dimensions={1} | concatenate | bytes 139264 | tf_op jit(solution)/shard_map/concatenate | solution.py:414
  3.2 35.0 %gather_all.1 = (bf16[4,2,2,2,16,2048]{5,4,3,2,1,0:T(8,128)(2,1)}, bf16[4,2,2,2,16,2176]{5,4,3,2,1,0:T(8,128)(2,1)}) custom-call(bf16[16,2048]{1,0:T(8,128)(2,1)} %own_a.1, bf16[16,2176]{1,0:T(8,128)(2,1)} %concatenate.3.own_b), custom_call_target="tpu_custom_call" | custom-call | tf_op jit(solution)/shard_map/gather_all/pallas_call | solution.py:251
  38.2 1.1 slice_convert_fusion
  39.3 0.1 copy.28
  39.4 0.1 copy.25
  39.5 0.1 fusion.1
  39.6 0.1 compare_reduce_fusion
  39.8 0.6 reshape.34.scale_row
  40.4 0.2 copy.27
  40.6 0.3 fusion.order_col
  40.8 0.0 copy-start.3
  40.8 0.7 copy.29.order_row
  41.6 0.0 copy-done.3
  41.6 0.0 copy-start.1
  41.6 35.6 %expert_rows.1 = (bf16[8,128,2048]{2,1,0:T(8,128)(2,1)}, bf16[8,128,2048]{2,1,0:T(8,128)(2,1)}, bf16[8,128,384]{2,1,0:T(8,128)(2,1)}, bf16[8,128,384]{2,1,0:T(8,...) custom-call(bf16[512,2048]{1,0:T(8,128)(2,1)} %bitcast.11, bf16[512,2176]{1,0:T(8,128)(2,1)} %bitcast.10, ...), custom_call_target="tpu_custom_call" | custom-call | flops 9663676416 | bytes 37748736 | tf_op jit(solution)/shard_map/expert_rows/pallas_call | solution.py:434
  77.2 0.0 copy-start.2
  77.2 2.2 %copy-done.2 = bf16[2,512,2048]{2,1,0:T(8,128)(2,1)S(1)} copy-done((bf16[2,512,2048]{2,1,0:T(8,128)(2,1)S(1)}, bf16[2,512,2048]{2,1,0:T(8,128)(2,1)}, u32[]{:S(2)}) %copy-start.2) | copy-done | bytes 4194328
  79.4 31.4 %reduce_all.1 = (bf16[16,2048]{1,0:T(8,128)(2,1)S(1)}, bf16[16,2048]{1,0:T(8,128)(2,1)S(1)}) custom-call(bf16[2,4,2,2,2,16,2048]{6,5,4,3,2,1,0:T(8,128)(2,1)S(1)} %bitcast.8), custom_call_target="tpu_custom_call" | custom-call | tf_op jit(solution)/shard_map/reduce_all/pallas_call | solution.py:315
  110.7 17.5 %expert_weights.1 = (bf16[8,2048,384]{2,1,0:T(8,128)(2,1)}, bf16[8,2048,384]{2,1,0:T(8,128)(2,1)}, bf16[8,384,2048]{2,1,0:T(8,128)(2,1)}) custom-call(bf16[8,128,2048]{2,1,0:T(8,128)(2,1)} %get-tuple-element.23.inputs, bf16[8,128,2048]{2,1,0:T(8,128)(2,1)} %get-tuple-element.24.cotangent, bf16[8,128,384]{2,1,0:T(8,128)(2,1)} %get-tuple-element.25.act, ...), custom_call_target="tpu_custom_call" | custom-call | flops 4831838208 | bytes 37748736 | tf_op jit(solution)/shard_map/expert_weights/pallas_call | solution.py:476
  128.3 0.6 copy.35
  128.9 0.6 copy.36
  129.5 0.0 copy-done.1
  (3 shorter events, 0.0 us)
Async XLA Ops:
  0.6 0.9 copy-start
  40.8 0.7 copy-start.3
  41.6 88.0 %copy-start.1 = (s32[64,8]{0,1:T(8,128)S(1)}, s32[64,8]{0,1:T(8,128)}, u32[]{:S(2)}) copy-start(s32[64,8]{0,1:T(8,128)} %param.9) | copy-start | bytes 6148
  77.2 2.2 %copy-start.2 = (bf16[2,512,2048]{2,1,0:T(8,128)(2,1)S(1)}, bf16[2,512,2048]{2,1,0:T(8,128)(2,1)}, u32[]{:S(2)}) copy-start(bf16[2,512,2048]{2,1,0:T(8,128)(2,1)} %get-tuple-element.20) | copy-start | bytes 12582916

commit v2 on v1

--- a/solution.py
+++ b/solution.py
@@ -218,25 +218,26 @@
             along[h, k] = start_send(own[h], here, *sems(0, h, k), away)
     for copy in stay:
         copy.wait()
-    for k in range(ring):
-        zz = lax.rem(z - k + ring, ring)
+    for step in range(ring + 2):
         for h in range(2):
-            if k > 0:
+            k = step
+            if 0 < k < ring:
                 along[h, k].wait_recv()
-                block = full[h].at[zz, x, y, c]
+                block = full[h].at[lax.rem(z - k + ring, ring), x, y, c]
                 first[h, k] = start_send(block, block, *sems(1, h, k), peers[h][0])
-    for k in range(ring):
-        zz = lax.rem(z - k + ring, ring)
         for h in range(2):
-            first[h, k].wait_recv()
-            block = full[h].at[zz, :, y, c] if h == 0 else full[h].at[zz, x, :, c]
-            second[h, k] = start_send(block, block, *sems(2, h, k), peers[h][1])
-    for k in range(ring):
-        zz = lax.rem(z - k + ring, ring)
+            k = step - 1
+            if 0 <= k < ring:
+                zz = lax.rem(z - k + ring, ring)
+                first[h, k].wait_recv()
+                block = full[h].at[zz, :, y, c] if h == 0 else full[h].at[zz, x, :, c]
+                second[h, k] = start_send(block, block, *sems(2, h, k), peers[h][1])
         for h in range(2):
-            second[h, k].wait_recv()
-            block = full[h].at[zz, :, :, c]
-            third[h, k] = start_send(block, block, *sems(3, h, k), at.core_peer())
+            k = step - 2
+            if 0 <= k < ring:
+                second[h, k].wait_recv()
+                block = full[h].at[lax.rem(z - k + ring, ring), :, :, c]
+                third[h, k] = start_send(block, block, *sems(3, h, k), at.core_peer())
     for copy in third.values():
         copy.wait_recv()
     for copies in (along, first, second, third):
@@ -277,18 +278,21 @@
         copies[0][h, k] = start_send(
             sums.at[h, aim[k], :, :, 1 - c], got1.at[h, k], *sems(0, h, k), at.core_peer()
         )
-    for k, h in pairs:
+
+    def fold_core(h, k):
         copies[0][h, k].wait_recv()
         sum1[h, k] = (sums[h, aim[k], :, :, c].astype(f32) + got1[h, k].astype(f32)).astype(bf16)
         part = sum1.at[h, k, :, 1 - y] if h == 0 else sum1.at[h, k, 1 - x]
         copies[1][h, k] = start_send(part, got2.at[h, k], *sems(1, h, k), peers[h][0])
-    for k, h in pairs:
+
+    def fold_first(h, k):
         copies[1][h, k].wait_recv()
         mine = sum1[h, k, :, y] if h == 0 else sum1[h, k, x]
         sum2[h, k] = (mine.astype(f32) + got2[h, k].astype(f32)).astype(bf16)
         part = sum2.at[h, k, 1 - x] if h == 0 else sum2.at[h, k, 1 - y]
         copies[2][h, k] = start_send(part, got3.at[h, k], *sems(2, h, k), peers[h][1])
-    for k, h in pairs:
+
+    def fold_second(h, k):
         copies[2][h, k].wait_recv()
         mine = sum2[h, k, x] if h == 0 else sum2[h, k, y]
         sum3[h, k] = (mine.astype(f32) + got3[h, k].astype(f32)).astype(bf16)
@@ -296,6 +300,12 @@
             copies[3][h, k] = start_send(
                 sum3.at[h, k], got4.at[h, k], *sems(3, h, k), at.device(z=aim[k])
             )
+
+    for step in range(ring + 2):
+        for late, fold in enumerate((fold_core, fold_first, fold_second)):
+            if 0 <= step - late < ring:
+                for h in range(2):
+                    fold(h, step - late)
     for h, out in enumerate((out_a, out_b)):
         total = sum3[h, ring - 1].astype(f32)
         for k in range(ring - 1):
@@ -323,7 +333,7 @@
             pltpu.SemaphoreType.DMA((4, 2, ring)),
         ],
         compiler_params=pltpu.CompilerParams(
-            collective_id=1, has_side_effects=True, vmem_limit_bytes=40 << 20
+            collective_id=1, has_side_effects=True, vmem_limit_bytes=60 << 20
         ),
         name="reduce_all",
     )(sums)
@@ -332,18 +342,35 @@
 def rows_kernel(
     tokens, grads, order_row, scale_row, order_col, gate_w, up_w, down_w,
     inputs_out, cotangent_out, act_out, gate_pre_out, up_pre_out, sums_out,
-    out_rows, in_rows,
+    out_rows, in_rows, all_inputs, all_cotangents,
 ):
     f32, bf16 = jnp.float32, jnp.bfloat16
     expert = pl.program_id(0)
     expert_count = order_col.shape[1]
     row_count = inputs_out.shape[1]
     token_count, width = tokens.shape
-    picked = select_rows(order_row[0], row_count)
+
+    @pl.when(expert == 0)
+    def _():
+        pick = jnp.concatenate(
+            [
+                jnp.where(select_rows(order_row[e], row_count), 1.0, 0.0).astype(bf16)
+                for e in range(expert_count)
+            ],
+            axis=0,
+        )
+        step = min(512, width)
+        for left in range(0, width, step):
+            for table, rows in ((tokens, all_inputs), (grads, all_cotangents)):
+                rows[:, left : left + step] = jnp.dot(
+                    pick, table[:, left : left + step], preferred_element_type=f32
+                ).astype(bf16)
+
+    here = pl.ds(pl.multiple_of(expert * row_count, row_count), row_count)
+    picked = select_rows(order_row[expert], row_count)
     row_scale = jnp.sum(jnp.where(picked, scale_row[0], 0.0), axis=1, keepdims=True)
-    pick = jnp.where(picked, 1.0, 0.0).astype(bf16)
-    inputs = jnp.dot(pick, tokens[...], preferred_element_type=f32).astype(bf16)
-    cotangent = jnp.dot(pick, grads[...], preferred_element_type=f32).astype(bf16)
+    inputs = all_inputs[here, :]
+    cotangent = all_cotangents[here, :]
     inputs_out[0] = inputs
     cotangent_out[0] = cotangent
     gate = jnp.dot(inputs, gate_w[0], preferred_element_type=f32)
@@ -359,7 +386,6 @@
     act_out[0] = act
     gate_pre_out[0] = gate_pre
     up_pre_out[0] = up_pre
-    here = pl.ds(pl.multiple_of(expert * row_count, row_count), row_count)
     out_rows[here, :] = jnp.dot(act, down_w[0], preferred_element_type=f32).astype(bf16)
     in_rows[here, :] = (
         lax.dot_general(gate_pre, gate_w[0], contract_last, preferred_element_type=f32)
@@ -437,7 +463,7 @@
         in_specs=[
             whole(total, width),
             whole(total, width),
-            each(1, total),
+            whole(experts, 1, total),
             each(1, total),
             whole(total, experts),
             each(width, hidden),
@@ -461,6 +487,8 @@
             jax.ShapeDtypeStruct((2, total, width), bf16),
         ],
         scratch_shapes=[
+            pltpu.VMEM((experts * row_count, width), bf16),
+            pltpu.VMEM((experts * row_count, width), bf16),
             pltpu.VMEM((experts * row_count, width), bf16),
             pltpu.VMEM((experts * row_count, width), bf16),
         ],

time: 130 us -> 128 us (0.985)
  local copies, waits for them, and re-layouts: 7.7 us -> 5.53 us
    unnamed x12 -> x14, local copies, waits for them, and re-layouts: 3.62 us -> 1.45 us
    pallas_call x1, Pallas kernels: 35 us -> 33.6 us  [gather_all(): pl.pallas_call(gather_kernel, in_specs=[anywhere, anywhere], out_specs=[a...]
where the time goes in v2:
time: 128 us
  Pallas kernels  120 us (94%)
  local copies, waits for them, and re-layouts  5.53 us (4%)
  other arithmetic  1.35 us (1%)
    pallas_call x1, Pallas kernels, gathered_shards(): pl.pallas_call(rows_kernel, grid=(experts,), in_specs=[whole(total, width...  36.7 us
    pallas_call x1, Pallas kernels, gather_all(): pl.pallas_call(gather_kernel, in_specs=[anywhere, anywhere], out_specs=[a...  33.6 us
    pallas_call x1, Pallas kernels, reduce_all(): pl.pallas_call(reduce_kernel, in_specs=[in_vmem], out_specs=[in_vmem, in_...  31.8 us
    pallas_call x1, Pallas kernels, gathered_shards(): pl.pallas_call(weights_kernel, grid=(experts,), in_specs=[each(row_count,...  17.6 us

profile of v2, /device:TPU:0, one launch (start us, length us, event | category | flops | bytes accessed | tf_op | source)
XLA Modules:
  0.0 127.5 jit_solution(17224529874734305382)
XLA Ops:
  0.6 0.0 copy-start
  0.7 0.8 constant_dynamic-slice_fusion
  1.4 0.1 copy.32
  1.5 0.0 copy-done
  1.5 0.1 constant_dynamic-slice_fusion.1
  1.6 0.1 copy.31
  1.7 1.6 %concatenate.3.own_b = bf16[16,2176]{1,0:T(8,128)(2,1)} concatenate(bf16[16,2048]{1,0:T(8,128)(2,1)} %param.8, bf16[16,8]{1,0:T(8,128)(2,1)S(1)} %convert_element_type.16, bf16[16,8]{1,0:T(8,128)(2,1)S(1)} %copy.32, bf16[16,112]{1,0:T(8,128)(2,1)S(1)} %broadcast_in_dim.24), dimensions={1} | concatenate | bytes 139264 | tf_op jit(solution)/shard_map/concatenate | solution.py:440
  3.2 33.6 %gather_all.1 = (bf16[4,2,2,2,16,2048]{5,4,3,2,1,0:T(8,128)(2,1)}, bf16[4,2,2,2,16,2176]{5,4,3,2,1,0:T(8,128)(2,1)}) custom-call(bf16[16,2048]{1,0:T(8,128)(2,1)} %own_a.1, bf16[16,2176]{1,0:T(8,128)(2,1)} %concatenate.3.own_b), custom_call_target="tpu_custom_call" | custom-call | tf_op jit(solution)/shard_map/gather_all/pallas_call | solution.py:252
  36.8 1.1 slice_convert_fusion
  37.9 0.1 copy.28
  38.0 0.1 copy.25
  38.1 0.1 fusion.1
  38.2 0.1 compare_reduce_fusion
  38.4 0.6 reshape.34.scale_row
  39.0 0.2 copy.27
  39.2 0.3 fusion.order_col
  39.4 0.0 copy-start.2
  39.5 0.7 copy.29.order_row
  40.2 0.0 copy-done.2
  40.2 0.0 copy-start.1
  40.2 36.7 %expert_rows.1 = (bf16[8,128,2048]{2,1,0:T(8,128)(2,1)}, bf16[8,128,2048]{2,1,0:T(8,128)(2,1)}, bf16[8,128,384]{2,1,0:T(8,128)(2,1)}, bf16[8,128,384]{2,1,0:T(8,...) custom-call(bf16[512,2048]{1,0:T(8,128)(2,1)} %bitcast.11, bf16[512,2176]{1,0:T(8,128)(2,1)} %bitcast.10, ...), custom_call_target="tpu_custom_call" | custom-call | flops 9663676416 | bytes 37748736 | tf_op jit(solution)/shard_map/expert_rows/pallas_call | solution.py:460
  76.9 31.8 %reduce_all.1 = (bf16[16,2048]{1,0:T(8,128)(2,1)}, bf16[16,2048]{1,0:T(8,128)(2,1)}) custom-call(bf16[2,4,2,2,2,16,2048]{6,5,4,3,2,1,0:T(8,128)(2,1)} %bitcast.8), custom_call_target="tpu_custom_call" | custom-call | tf_op jit(solution)/shard_map/reduce_all/pallas_call | solution.py:325
  108.7 0.0 copy-start.4
  108.7 0.0 copy-start.3
  108.7 17.6 %expert_weights.1 = (bf16[8,2048,384]{2,1,0:T(8,128)(2,1)}, bf16[8,2048,384]{2,1,0:T(8,128)(2,1)}, bf16[8,384,2048]{2,1,0:T(8,128)(2,1)}) custom-call(bf16[8,128,2048]{2,1,0:T(8,128)(2,1)} %get-tuple-element.23.inputs, bf16[8,128,2048]{2,1,0:T(8,128)(2,1)} %get-tuple-element.24.cotangent, bf16[8,128,384]{2,1,0:T(8,128)(2,1)} %get-tuple-element.25.act, ...), custom_call_target="tpu_custom_call" | custom-call | flops 4831838208 | bytes 37748736 | tf_op jit(solution)/shard_map/expert_weights/pallas_call | solution.py:504
  126.3 0.0 copy-done.4
  126.3 0.6 copy.35
  126.9 0.0 copy-done.3
  126.9 0.6 copy.36
  127.5 0.0 copy-done.1
  (3 shorter events, 0.0 us)
Async XLA Ops:
  0.6 0.9 copy-start
  39.4 0.7 copy-start.2
  40.2 87.4 %copy-start.1 = (s32[64,8]{0,1:T(8,128)S(1)}, s32[64,8]{0,1:T(8,128)}, u32[]{:S(2)}) copy-start(s32[64,8]{0,1:T(8,128)} %param.9) | copy-start | bytes 6148
  108.7 17.6 %copy-start.4 = (bf16[16,2048]{1,0:T(8,128)(2,1)S(1)}, bf16[16,2048]{1,0:T(8,128)(2,1)}, u32[]{:S(2)}) copy-start(bf16[16,2048]{1,0:T(8,128)(2,1)} %get-tuple-element.38) | copy-start | bytes 196612
  108.7 18.2 %copy-start.3 = (bf16[16,2048]{1,0:T(8,128)(2,1)S(1)}, bf16[16,2048]{1,0:T(8,128)(2,1)}, u32[]{:S(2)}) copy-start(bf16[16,2048]{1,0:T(8,128)(2,1)} %get-tuple-element.39) | copy-start | bytes 196612
